TPU v7x, 32 devices: a whole 2x2x4 slice. The times are simulated.
32 devices in a mesh: seg: 4 (over z), mem: 8 (over y, x, core).
Axes of the slice: x: 2, y: 2, z: 4, core: 2. Of those that a mesh axis runs over, the one named last changes fastest.
Arguments:
- tokens: bfloat16 [8192, 1024], P(('seg', 'mem')), may hold values from -6 to 6
- padding_mask: int32 [8192], P(('seg', 'mem')), may hold values from 0 to 1, as said below
- memory_keys: bfloat16 [4, 8192, 1024], P('seg', 'mem'), may hold values from -6 to 6
- memory_values: bfloat16 [4, 8192, 1024], P('seg', 'mem'), may hold values from -6 to 6
- memory_length: int32 [4], P('seg'), may hold values from 2048 to 8192, as said below
- chosen_keys: int32 [16, 128], P('seg'), may hold values from 0 to 8191, as said below
- norm_gain: float32 [1024], replicated, may hold values from 0.1 to 1.9
- w_query: bfloat16 [1024, 1024], replicated, may hold values from -0.1875 to 0.1875
- w_key: bfloat16 [1024, 1024], replicated, may hold values from -0.1875 to 0.1875
- w_value: bfloat16 [1024, 1024], replicated, may hold values from -0.1875 to 0.1875
- w_out: bfloat16 [1024, 1024], replicated, may hold values from -1.5 to 1.5
- ffn_gain: float32 [1024], replicated, may hold values from 0.1 to 1.9
- w_gate: bfloat16 [1024, 2816], replicated, may hold values from -0.1875 to 0.1875
- w_up: bfloat16 [1024, 2816], replicated, may hold values from -0.1875 to 0.1875
- w_down: bfloat16 [2816, 1024], replicated, may hold values from -0.109375 to 0.109375
- cotangent: bfloat16 [8192, 1024], P(('seg', 'mem')), may hold values from -6 to 6
Outputs:
- mixed: bfloat16 [8192, 1024], P(('seg', 'mem'))
- input_grad: bfloat16 [8192, 1024], P(('seg', 'mem'))
- norm_gain_grad: float32 [1024], P('mem')
- query_grad: float32 [1024, 1024], P('mem')
- key_grad: float32 [1024, 1024], P('mem')
- value_grad: float32 [1024, 1024], P('mem')
- out_grad: float32 [1024, 1024], P('mem')
- ffn_gain_grad: float32 [1024], P('mem')
- gate_grad: float32 [1024, 2816], P('mem')
- up_grad: float32 [1024, 2816], P('mem')
- down_grad: float32 [2816, 1024], P('mem')
Inputs may be any that keep to these rules, and one draw needn't show every extreme that they name: `padding_mask`: within each segment of 2048 consecutive tokens the ones form a prefix of 1024 tokens or more. `memory_length`: how many of a segment's 8192 memory slots are live. `chosen_keys`: row b belongs to the queries b * 512 to (b + 1) * 512 - 1; its first entry is below 2048.
All inputs are finite; a program needn't handle non-finite values.
Results may differ from a plain program's by a relative error of at most 0.014.
Values may be sent and summed in bfloat16 or wider, within the bound.
No kernel may reach another device: no remote copies, remote signals or barrier semaphores. Data moves between devices by JAX's collectives and lax.ppermute only.
A program may use at most 320 MiB of HBM per device.

v0:
```python
import math
import jax
import jax.numpy as jnp
from jax import lax
from jax.sharding import PartitionSpec as P

H = 8
HD = 128
SEG_LEN = 2048
QB = 512
TOPK = 128
EPSILON = 1e-05
NEGATIVE = -1e30


def outer_product(left, right):
    return lax.dot_general(
        left, right, (((0,), (0,)), ((), ())), preferred_element_type=jnp.float32
    )


def backward_dot(left, weight):
    return lax.dot_general(
        left, weight, (((1,), (1,)), ((), ())), preferred_element_type=jnp.float32
    )


def forward_dot(left, weight):
    return jnp.dot(left, weight, preferred_element_type=jnp.float32)


def normalize(values):
    factor = lax.rsqrt(jnp.mean(values * values, axis=-1, keepdims=True) + EPSILON)
    return (values * factor, factor)


def norm_back(grad_in, normed, factor, gain):
    scaled = grad_in * gain
    return factor * (scaled - normed * jnp.mean(scaled * normed, axis=-1, keepdims=True))


def block_stats(scores, usable):
    highest = jnp.max(scores, axis=-1)
    row_sum = jnp.sum(jnp.where(usable, jnp.exp(scores - highest[..., None]), 0.0), axis=-1)
    return (highest, row_sum)


def join_stats(high_left, sum_left, high_right, sum_right):
    highest = jnp.maximum(high_left, high_right)
    return (
        highest,
        sum_left * jnp.exp(high_left - highest) + sum_right * jnp.exp(high_right - highest),
    )


def local(
    tokens,
    padding_mask,
    memory_keys,
    memory_values,
    memory_length,
    chosen_keys,
    norm_gain,
    w_query,
    w_key,
    w_value,
    w_out,
    ffn_gain,
    w_gate,
    w_up,
    w_down,
    cotangent,
):
    group_size = lax.axis_size("mem")
    position = lax.axis_index("mem")
    tok_rows, model_width = tokens.shape
    memory_rows = memory_keys.shape[1]
    segment_count = memory_keys.shape[0]
    all_rows = tok_rows * group_size
    blocks = all_rows // QB
    segment_blocks = SEG_LEN // QB
    score_scale = 1.0 / math.sqrt(HD)
    inputs = tokens.astype(jnp.float32)
    normed_one, factor_one = normalize(inputs)
    h_one = (normed_one * norm_gain).astype(jnp.bfloat16)
    queries = forward_dot(h_one, w_query).astype(jnp.bfloat16)
    keyed_flat = forward_dot(h_one, w_key).astype(jnp.bfloat16)
    valued_flat = forward_dot(h_one, w_value).astype(jnp.bfloat16)
    own_keys = keyed_flat.reshape(tok_rows, H, HD)
    own_values = valued_flat.reshape(tok_rows, H, HD)
    first_row = position * tok_rows
    own_segment = first_row // SEG_LEN
    own_offset = first_row % SEG_LEN
    start_block = own_segment * segment_blocks
    key_position = own_offset + jnp.arange(tok_rows)
    key_usable = padding_mask == 1
    block_segment = jnp.arange(blocks) * QB // SEG_LEN
    segment_match = block_segment[:, None] == jnp.arange(segment_count)[None, :]
    limits = jnp.sum(jnp.where(segment_match, memory_length[None, :], 0), axis=1)
    shifted = chosen_keys - position * memory_rows
    owned = (shifted >= 0) & (shifted < memory_rows) & (chosen_keys < limits[:, None])
    columns = jnp.arange(memory_rows)

    def select_slots(pieces):
        local_rows, usable, segment = pieces
        table = ((local_rows[:, None] == columns[None, :]) & usable[:, None]).astype(jnp.bfloat16)
        keys_here = lax.dynamic_index_in_dim(memory_keys, segment, 0, keepdims=False)
        values_here = lax.dynamic_index_in_dim(memory_values, segment, 0, keepdims=False)
        return (
            forward_dot(table, keys_here).astype(jnp.bfloat16),
            forward_dot(table, values_here).astype(jnp.bfloat16),
        )

    picked_keys, picked_values = lax.map(select_slots, (shifted, owned, block_segment))
    gathered = lax.all_gather(queries, "mem", axis=0, tiled=True).reshape(blocks, QB, H, HD)
    picked_keys = picked_keys.reshape(blocks, TOPK, H, HD)
    picked_values = picked_values.reshape(blocks, TOPK, H, HD)

    def memory_scores(query_block, key_block, usable):
        scores = (
            jnp.einsum("qhd,thd->qht", query_block, key_block, preferred_element_type=jnp.float32)
            * score_scale
        )
        return jnp.where(usable[None, None, :], scores, NEGATIVE)

    def local_visible(block_index):
        query_position = block_index * QB + jnp.arange(QB)
        return (key_position[None, :] <= query_position[:, None]) & key_usable[None, :]

    def local_scores(query_block, visible):
        scores = (
            jnp.einsum("qhd,khd->qhk", query_block, own_keys, preferred_element_type=jnp.float32)
            * score_scale
        )
        return jnp.where(visible[:, None, :], scores, NEGATIVE)

    def segment_rows(source, block_index):
        return lax.dynamic_index_in_dim(source, start_block + block_index, 0, keepdims=False)

    def add_segment(whole, local_part):
        merged = lax.dynamic_slice_in_dim(whole, start_block, segment_blocks, 0) + local_part
        return lax.dynamic_update_slice_in_dim(whole, merged, start_block, 0)

    def memory_first(pieces):
        query_block, key_block, usable = pieces
        return block_stats(memory_scores(query_block, key_block, usable), usable[None, None, :])

    memory_high, memory_sum = lax.map(memory_first, (gathered, picked_keys, owned))

    def local_first(block_index):
        visible = local_visible(block_index)
        scores = local_scores(segment_rows(gathered, block_index), visible)
        return block_stats(scores, visible[:, None, :])

    local_high, local_sum = lax.map(local_first, jnp.arange(segment_blocks))
    seg_high = lax.dynamic_slice_in_dim(memory_high, start_block, segment_blocks, 0)
    seg_sum = lax.dynamic_slice_in_dim(memory_sum, start_block, segment_blocks, 0)
    seg_high, seg_sum = join_stats(seg_high, seg_sum, local_high, local_sum)
    memory_high = lax.dynamic_update_slice_in_dim(memory_high, seg_high, start_block, 0)
    memory_sum = lax.dynamic_update_slice_in_dim(memory_sum, seg_sum, start_block, 0)
    row_high = lax.pmax(memory_high.astype(jnp.bfloat16), "mem").astype(memory_high.dtype)
    row_sum = lax.psum(memory_sum * jnp.exp(memory_high - row_high), "mem")
    log_total = row_high + jnp.log(row_sum)

    def memory_second(pieces):
        query_block, key_block, value_block, usable, block_total = pieces
        scores = memory_scores(query_block, key_block, usable)
        weights = jnp.where(
            usable[None, None, :], jnp.exp(scores - block_total[..., None]), 0.0
        ).astype(jnp.bfloat16)
        return jnp.einsum("qht,thd->qhd", weights, value_block, preferred_element_type=jnp.float32)

    numerators = lax.map(memory_second, (gathered, picked_keys, picked_values, owned, log_total))

    def local_second(block_index):
        visible = local_visible(block_index)
        scores = local_scores(segment_rows(gathered, block_index), visible)
        block_total = segment_rows(log_total, block_index)
        weights = jnp.where(
            visible[:, None, :], jnp.exp(scores - block_total[..., None]), 0.0
        ).astype(jnp.bfloat16)
        return jnp.einsum("qhk,khd->qhd", weights, own_values, preferred_element_type=jnp.float32)

    numerators = add_segment(numerators, lax.map(local_second, jnp.arange(segment_blocks)))
    attended_sum = lax.psum_scatter(
        numerators.reshape(all_rows, model_width), "mem", scatter_dimension=0, tiled=True
    )
    attended = attended_sum.astype(jnp.bfloat16)
    residual = inputs + forward_dot(attended, w_out)
    normed_two, factor_two = normalize(residual)
    h_two = (normed_two * ffn_gain).astype(jnp.bfloat16)
    gate = forward_dot(h_two, w_gate)
    up_part = forward_dot(h_two, w_up)
    sigmoid_gate = jax.nn.sigmoid(gate)
    silu_gate = gate * sigmoid_gate
    act = (silu_gate * up_part).astype(jnp.bfloat16)
    mixed = (residual + forward_dot(act, w_down)).astype(jnp.bfloat16)
    down_grad = outer_product(act, cotangent)
    d_act = backward_dot(cotangent, w_down)
    d_gate = (d_act * up_part * sigmoid_gate * (1.0 + gate * (1.0 - sigmoid_gate))).astype(
        jnp.bfloat16
    )
    d_up = (d_act * silu_gate).astype(jnp.bfloat16)
    gate_grad = outer_product(h_two, d_gate)
    up_grad = outer_product(h_two, d_up)
    d_two = backward_dot(d_gate, w_gate) + backward_dot(d_up, w_up)
    ffn_gain_grad = jnp.sum(d_two * normed_two, axis=0)
    d_res = cotangent.astype(jnp.float32) + norm_back(d_two, normed_two, factor_two, ffn_gain)
    d_res_low = d_res.astype(jnp.bfloat16)
    out_grad = outer_product(attended, d_res_low)
    d_att = backward_dot(d_res_low, w_out).astype(jnp.bfloat16)
    grad_rows = lax.all_gather(d_att, "mem", axis=0, tiled=True).reshape(blocks, QB, H, HD)

    def memory_third(pieces):
        query_block, key_block, value_block, usable, block_total, grad_block = pieces
        scores = memory_scores(query_block, key_block, usable)
        probs = jnp.where(usable[None, None, :], jnp.exp(scores - block_total[..., None]), 0.0)
        pushes = jnp.einsum(
            "qhd,thd->qht", grad_block, value_block, preferred_element_type=jnp.float32
        )
        return jnp.sum(probs * pushes, axis=-1)

    delta_part = lax.map(
        memory_third, (gathered, picked_keys, picked_values, owned, log_total, grad_rows)
    )

    def local_third(block_index):
        visible = local_visible(block_index)
        scores = local_scores(segment_rows(gathered, block_index), visible)
        block_total = segment_rows(log_total, block_index)
        probs = jnp.where(visible[:, None, :], jnp.exp(scores - block_total[..., None]), 0.0)
        pushes = jnp.einsum(
            "qhd,khd->qhk",
            segment_rows(grad_rows, block_index),
            own_values,
            preferred_element_type=jnp.float32,
        )
        return jnp.sum(probs * pushes, axis=-1)

    delta_part = add_segment(delta_part, lax.map(local_third, jnp.arange(segment_blocks)))
    delta = lax.psum(delta_part, "mem")

    def memory_fourth(pieces):
        query_block, key_block, value_block, usable, block_total, grad_block, block_delta = pieces
        scores = memory_scores(query_block, key_block, usable)
        probs = jnp.where(usable[None, None, :], jnp.exp(scores - block_total[..., None]), 0.0)
        pushes = jnp.einsum(
            "qhd,thd->qht", grad_block, value_block, preferred_element_type=jnp.float32
        )
        d_scores = jnp.where(
            usable[None, None, :], probs * (pushes - block_delta[..., None]), 0.0
        ).astype(jnp.bfloat16)
        return (
            jnp.einsum("qht,thd->qhd", d_scores, key_block, preferred_element_type=jnp.float32)
            * score_scale
        )

    query_terms = lax.map(
        memory_fourth, (gathered, picked_keys, picked_values, owned, log_total, grad_rows, delta)
    )

    def local_fourth(running, block_index):
        key_acc, value_acc = running
        visible = local_visible(block_index)
        query_block = segment_rows(gathered, block_index)
        grad_block = segment_rows(grad_rows, block_index)
        scores = local_scores(query_block, visible)
        block_total = segment_rows(log_total, block_index)
        block_delta = segment_rows(delta, block_index)
        probs = jnp.where(visible[:, None, :], jnp.exp(scores - block_total[..., None]), 0.0)
        pushes = jnp.einsum(
            "qhd,khd->qhk", grad_block, own_values, preferred_element_type=jnp.float32
        )
        d_scores = jnp.where(
            visible[:, None, :], probs * (pushes - block_delta[..., None]), 0.0
        ).astype(jnp.bfloat16)
        query_term = (
            jnp.einsum("qhk,khd->qhd", d_scores, own_keys, preferred_element_type=jnp.float32)
            * score_scale
        )
        key_acc = (
            key_acc
            + jnp.einsum("qhk,qhd->khd", d_scores, query_block, preferred_element_type=jnp.float32)
            * score_scale
        )
        value_acc = value_acc + jnp.einsum(
            "qhk,qhd->khd",
            probs.astype(jnp.bfloat16),
            grad_block,
            preferred_element_type=jnp.float32,
        )
        return ((key_acc, value_acc), query_term)

    empty_acc = jnp.zeros((tok_rows, H, HD), jnp.float32)
    (key_sum, value_sum), local_terms = lax.scan(
        local_fourth, (empty_acc, empty_acc), jnp.arange(segment_blocks)
    )
    query_terms = add_segment(query_terms, local_terms)
    d_query = lax.psum_scatter(
        query_terms.reshape(all_rows, model_width), "mem", scatter_dimension=0, tiled=True
    ).astype(jnp.bfloat16)
    d_key = key_sum.reshape(tok_rows, model_width).astype(jnp.bfloat16)
    d_value = value_sum.reshape(tok_rows, model_width).astype(jnp.bfloat16)
    query_grad = outer_product(h_one, d_query)
    key_grad = outer_product(h_one, d_key)
    value_grad = outer_product(h_one, d_value)
    d_one = (
        backward_dot(d_query, w_query) + backward_dot(d_key, w_key) + backward_dot(d_value, w_value)
    )
    norm_gain_grad = jnp.sum(d_one * normed_one, axis=0)
    input_grad = (d_res + norm_back(d_one, normed_one, factor_one, norm_gain)).astype(jnp.bfloat16)
    shards = (
        lax.psum_scatter(norm_gain_grad, "mem", scatter_dimension=0, tiled=True),
        lax.psum_scatter(query_grad, "mem", scatter_dimension=0, tiled=True),
        lax.psum_scatter(key_grad, "mem", scatter_dimension=0, tiled=True),
        lax.psum_scatter(value_grad, "mem", scatter_dimension=0, tiled=True),
        lax.psum_scatter(out_grad, "mem", scatter_dimension=0, tiled=True),
        lax.psum_scatter(ffn_gain_grad, "mem", scatter_dimension=0, tiled=True),
        lax.psum_scatter(gate_grad, "mem", scatter_dimension=0, tiled=True),
        lax.psum_scatter(up_grad, "mem", scatter_dimension=0, tiled=True),
        lax.psum_scatter(down_grad, "mem", scatter_dimension=0, tiled=True),
    )
    (
        norm_part,
        query_part,
        key_part,
        value_part,
        out_part,
        ffn_gain_part,
        gate_part,
        up_grad_part,
        down_part,
    ) = shards
    summed = lax.psum(
        (
            norm_part,
            query_part,
            key_part,
            value_part,
            out_part,
            ffn_gain_part,
            gate_part,
            up_grad_part,
            down_part,
        ),
        "seg",
    )
    (
        norm_done,
        query_done,
        key_done,
        value_done,
        out_done,
        ffn_gain_done,
        gate_done,
        up_done,
        down_done,
    ) = summed
    return (
        mixed,
        input_grad,
        norm_done,
        query_done,
        key_done,
        value_done,
        out_done,
        ffn_gain_done,
        gate_done,
        up_done,
        down_done,
    )


def solution(mesh):
    return jax.shard_map(
        local,
        mesh=mesh,
        in_specs=(
            P(("seg", "mem"), None),
            P(("seg", "mem")),
            P("seg", "mem", None),
            P("seg", "mem", None),
            P("seg"),
            P("seg", None),
            P(),
            P(),
            P(),
            P(),
            P(),
            P(),
            P(),
            P(),
            P(),
            P(("seg", "mem"), None),
        ),
        out_specs=(
            P(("seg", "mem"), None),
            P(("seg", "mem"), None),
            P("mem"),
            P("mem", None),
            P("mem", None),
            P("mem", None),
            P("mem", None),
            P("mem"),
            P("mem", None),
            P("mem", None),
            P("mem", None),
        ),
        check_vma=False,
    )
```

profile of v0, /device:TPU:0, one launch (start us, length us, event | category | flops | bytes accessed | tf_op | source)
XLA Modules:
  0.0 1458.7 jit_solution(2463133091801142676)
XLA Ops:
  8.7 3.3 convolution_convert_fusion.3
  15.4 22.5 %while.110 = (s32[]{:T(128)}, bf16[4,128,1024]{2,1,0:T(8,128)(2,1)}, bf16[4,128,1024]{2,1,0:T(8,128)(2,1)}, s32[4,128]{1,0:T(4,128)S(1)}, pred[4,128]{1,0:T(4,12...) while((s32[]{:T(128)}, bf16[4,128,1024]{2,1,0:T(8,128)(2,1)}, ...), condition=%wide.region_2.3_spmd.clone, body=%wide.region_1.2_spmd.clone.sunk | while | flops 537657344 | bytes 4721261 | solution.py:114
  40.4 11.2 all-gather.3.cloned.1.call-done
  51.6 3.3 copy.139
  57.8 20.9 %while.111 = (s32[]{:T(128)}, f32[4,512,8]{1,2,0:T(8,128)S(1)}, f32[4,512,8]{1,2,0:T(8,128)S(1)}, s32[4]{0:T(128)S(1)}, pred[256]{0:T(512)(128)(4,1)S(1)}, /*ind...) while((s32[]{:T(128)}, f32[4,512,8]{1,2,0:T(8,128)S(1)}, ...), condition=%wide.region_10.11_spmd.clone, body=%wide.region_7.10_spmd.clone.sunk | while | flops 277078784 | bytes 10475995 | solution.py:155
  78.8 9.8 while.106
  88.6 23.5 %pmax.7 = bf16[4,512,8]{1,2,0:T(8,128)(2,1)S(1)} all-reduce(bf16[4,512,8]{1,2,0:T(8,128)(2,1)S(1)} %get-tuple-element.1010), channel_id=1, replica_groups=mesh['seg'=4,'mem'=8] {'mem'}, use_global_device_ids=true, to_apply=%region_11.12 | all-reduce | flops 16384 | bytes 65536 | tf_op jit(solution)/shard_map/pmax | solution.py:161
  119.1 46.3 %all-reduce.9.cloned.1.call-done = f32[4,512,8]{1,2,0:T(8,128)} async-done(((f32[4,512,8]{1,2,0:T(8,128)}), f32[4,512,8]{1,2,0:T(8,128)}) %all-reduce.9.cloned.1.call-update) | async-done | bytes 65552 | tf_op jit(solution)/shard_map/psum | solution.py:162
  166.3 4.2 broadcast.311.clone3.1
  170.5 26.2 %while.112 = (s32[]{:T(128)}, f32[4,512,8,128]{3,1,2,0:T(8,128)}, s32[4]{0:T(128)S(1)}, pred[256]{0:T(512)(128)(4,1)S(1)}, s32[]{:T(128)}, /*index=5*/bf16[4,512...) while((s32[]{:T(128)}, f32[4,512,8,128]{3,1,2,0:T(8,128)}, ...), condition=%wide.region_16.17_spmd.clone, body=%wide.region_15.16_spmd.clone.sunk | while | flops 542376704 | bytes 4643303 | solution.py:184
  172.6 4.4 bitcast_dynamic-update-slice_fusion.17
  179.2 4.4 bitcast_dynamic-update-slice_fusion.17
  185.7 4.5 bitcast_dynamic-update-slice_fusion.17
  192.3 4.5 bitcast_dynamic-update-slice_fusion.17
  196.8 4.2 broadcast.311.clone3
  201.0 46.6 %while.107 = (s32[]{:T(128)}, f32[4,512,8,128]{3,1,2,0:T(8,128)}, bf16[4,128,8,128]{3,2,1,0:T(8,128)(2,1)}, pred[4,128]{1,0:T(4,128)(4,1)S(1)}, bf16[4,128,8,128...) while((s32[]{:T(128)}, f32[4,512,8,128]{3,1,2,0:T(8,128)}, ...), condition=%wide.region_14.15_spmd, body=%wide.region_13.14_spmd.sunk | while | flops 271056896 | bytes 13158765 | solution.py:173
  202.9 3.6 convolution_bitcast_fusion.2
  214.4 3.6 convolution_bitcast_fusion.2
  225.9 3.6 convolution_bitcast_fusion.2
  237.4 3.6 convolution_bitcast_fusion.2
  247.5 10.3 add.250
  257.8 8.2 copy.98
  266.1 5.3 copy.150
  271.5 70.8 %reduce-scatter.10.cloned.1.call-done = f32[256,1024]{1,0:T(8,128)} async-done(((f32[2048,1024]{1,0:T(8,128)}), f32[256,1024]{1,0:T(8,128)}) %reduce-scatter.10.cloned.1.call-update) | async-done | bytes 1048592 | tf_op jit(solution)/shard_map/reduce_scatter | solution.py:185
  345.4 6.3 fusion.216
  351.7 3.3 fusion.215
  355.0 5.9 multiply_convert_fusion
  370.4 34.3 %all-gather.5.cloned.1.call-done = bf16[2048,1024]{1,0:T(8,128)(2,1)} async-done(((bf16[256,1024]{1,0:T(8,128)(2,1)}), bf16[2048,1024]{1,0:T(8,128)(2,1)}) %all-gather.5.cloned.1.call-update) | async-done | bytes 4194320 | tf_op jit(solution)/shard_map/all_gather | solution.py:212
  404.7 3.3 copy.141
  410.9 28.1 %while.113 = (s32[]{:T(128)}, f32[4,512,8]{1,2,0:T(8,128)S(1)}, s32[4]{0:T(128)S(1)}, pred[256]{0:T(512)(128)(4,1)S(1)}, s32[]{:T(128)}, /*index=5*/bf16[4,512,8...) while((s32[]{:T(128)}, f32[4,512,8]{1,2,0:T(8,128)S(1)}, ...), condition=%wide.region_25.26_spmd.clone, body=%wide.region_23.25_spmd.clone.sunk | while | flops 543421184 | bytes 12032499 | solution.py:240
  439.0 15.7 %while.108 = (s32[]{:T(128)}, f32[4,512,8]{1,2,0:T(8,128)S(1)}, pred[4,128]{1,0:T(4,128)(4,1)S(1)}, bf16[4,128,8,128]{3,1,2,0:T(8,128)(2,1)}, bf16[4,512,8,128]{...) while((s32[]{:T(128)}, f32[4,512,8]{1,2,0:T(8,128)S(1)}, ...), condition=%wide.region_22.23_spmd, body=%wide.region_20.22_spmd.sunk | while | flops 271577088 | bytes 6917489 | solution.py:223
  455.5 52.6 %all-reduce.11.cloned.1.call-done = f32[4,512,8]{1,2,0:T(8,128)} async-done(((f32[4,512,8]{1,2,0:T(8,128)}), f32[4,512,8]{1,2,0:T(8,128)}) %all-reduce.11.cloned.1.call-update) | async-done | bytes 65552 | tf_op jit(solution)/shard_map/psum | solution.py:241
  508.1 4.2 broadcast.311.clone3.2
  512.3 55.4 %while.109 = (s32[]{:T(128)}, f32[4,512,8,128]{3,1,2,0:T(8,128)}, bf16[4,128,8,128]{3,1,2,0:T(8,128)(2,1)}, pred[4,128]{1,0:T(4,128)(4,1)S(1)}, bf16[4,512,8,128...) while((s32[]{:T(128)}, f32[4,512,8,128]{3,1,2,0:T(8,128)}, ...), condition=%wide.region_28.29_spmd, body=%wide.region_27.28_spmd.sunk | while | flops 407371776 | bytes 17665912 | solution.py:258
  515.6 4.6 multiply_bitcast_fusion.2
  526.3 3.1 fusion.329
  529.4 4.6 multiply_bitcast_fusion.2
  540.1 3.1 fusion.329
  543.3 4.6 multiply_bitcast_fusion.2
  553.9 3.1 fusion.329
  557.0 4.6 multiply_bitcast_fusion.2
  567.6 4.2 broadcast.311.clone3.3
  571.9 50.7 %while.114 = (s32[]{:T(128)}, f32[256,8,128]{0,2,1:T(8,128)}, f32[256,8,128]{0,2,1:T(8,128)}, f32[4,512,8,128]{3,1,2,0:T(8,128)}, s32[4]{0:T(128)S(1)}, /*index=...) while((s32[]{:T(128)}, f32[256,8,128]{0,2,1:T(8,128)}, ...), condition=%wide.region_30.31_spmd.clone, body=%wide.region_29.30_spmd.clone.sunk | while | flops 1357906688 | bytes 65264296 | solution.py:295
  622.6 10.3 add.259
  632.9 8.2 copy.117
  641.1 5.4 copy.149
  646.6 4.4 fusion.199
  652.7 3.2 fusion.206
  661.5 7.7 fusion.219
  669.2 7.4 fusion.218
  676.7 7.6 fusion.220
  684.4 33.0 %reduce-scatter.12.cloned.1.call-done = f32[256,1024]{1,0:T(8,128)} async-done(((f32[2048,1024]{1,0:T(8,128)}), f32[256,1024]{1,0:T(8,128)}) %reduce-scatter.12.cloned.1.call-update) | async-done | bytes 1048592 | tf_op jit(solution)/shard_map/reduce_scatter | solution.py:299
  717.4 4.0 fusion.195
  721.5 50.6 %reduce-scatter.20.cloned.1.call-done = f32[128,1024]{1,0:T(8,128)} async-done(((f32[1024,1024]{1,0:T(8,128)}), f32[128,1024]{1,0:T(8,128)}) %reduce-scatter.20.cloned.1.call-update) | async-done | bytes 524304 | tf_op jit(solution)/shard_map/reduce_scatter | solution.py:317
  772.1 55.1 %reduce-scatter.18.cloned.1.call-done = f32[128,1024]{1,0:T(8,128)} async-done(((f32[1024,1024]{1,0:T(8,128)}), f32[128,1024]{1,0:T(8,128)}) %reduce-scatter.18.cloned.1.call-update) | async-done | bytes 524304 | tf_op jit(solution)/shard_map/reduce_scatter | solution.py:316
  827.2 54.7 %reduce-scatter.16.cloned.1.call-done = f32[128,1024]{1,0:T(8,128)} async-done(((f32[1024,1024]{1,0:T(8,128)}), f32[128,1024]{1,0:T(8,128)}) %reduce-scatter.16.cloned.1.call-update) | async-done | bytes 524304 | tf_op jit(solution)/shard_map/reduce_scatter | solution.py:315
  881.9 90.6 %reduce-scatter.24.cloned.1.call-done = f32[128,2816]{1,0:T(8,128)} async-done(((f32[1024,2816]{1,0:T(8,128)}), f32[128,2816]{1,0:T(8,128)}) %reduce-scatter.24.cloned.1.call-update) | async-done | bytes 1441808 | tf_op jit(solution)/shard_map/reduce_scatter | solution.py:320
  972.4 90.7 %reduce-scatter.22.cloned.1.call-done = f32[128,2816]{1,0:T(8,128)} async-done(((f32[1024,2816]{1,0:T(8,128)}), f32[128,2816]{1,0:T(8,128)}) %reduce-scatter.22.cloned.1.call-update) | async-done | bytes 1441808 | tf_op jit(solution)/shard_map/reduce_scatter | solution.py:319
  1063.1 90.5 %reduce-scatter.26.cloned.1.call-done = f32[352,1024]{1,0:T(8,128)} async-done(((f32[2816,1024]{1,0:T(8,128)}), f32[352,1024]{1,0:T(8,128)}) %reduce-scatter.26.cloned.1.call-update) | async-done | bytes 1441808 | tf_op jit(solution)/shard_map/reduce_scatter | solution.py:321
  1153.7 55.0 %reduce-scatter.14.cloned.1.call-done = f32[128,1024]{1,0:T(8,128)} async-done(((f32[1024,1024]{1,0:T(8,128)}), f32[128,1024]{1,0:T(8,128)}) %reduce-scatter.14.cloned.1.call-update) | async-done | bytes 524304 | tf_op jit(solution)/shard_map/reduce_scatter | solution.py:314
  1210.0 5.9 fusion.184
  1221.0 13.1 all-reduce.2
  1234.3 12.5 all-reduce.3
  1249.5 191.5 %all-reduce.13.cloned.1.call-done = (f32[128,1024]{1,0:T(8,128)}, f32[128,1024]{1,0:T(8,128)}, f32[128,1024]{1,0:T(8,128)}, f32[128,1024]{1,0:T(8,128)}, f32[128...) async-done(((f32[128,1024]{1,0:T(8,128)}, f32[128,1024]{1,0:T(8,128)}, f32[128,1024]{1,0:T(8,128)}, f32[128,1024]{1,0:T(8,128)}, f32[128,2816]{1,0:T(8,128)}, ...) | async-done | bytes 6422544 | tf_op jit(solution)/shard_map/psum | solution.py:334
  (413 shorter events, 252.7 us)
Async XLA Ops:
  7.2 106.0 %copy-start = (bf16[1024,1024]{1,0:T(8,128)(2,1)S(1)}, bf16[1024,1024]{1,0:T(8,128)(2,1)}, u32[]{:S(2)}) copy-start(bf16[1024,1024]{1,0:T(8,128)(2,1)} %param.43) | copy-start | bytes 6291460
  7.2 5.6 copy-start.3
  7.2 5.6 copy-start.25
  7.2 44.4 %all-gather.3.cloned.1.call-start = ((), (), s32[]{:S(2)}) async-start(), calls=%async_computation.9 | async-start | bytes 4718592 | tf_op jit(solution)/shard_map/all_gather | solution.py:115
  8.6 104.5 %copy-start.27 = (f32[256]{0:T(256)}, f32[256]{0:T(256)S(1)}, u32[]{:S(2)}) copy-start(f32[256]{0:T(256)S(1)} %add_rsqrt_fusion.1) | copy-start | bytes 3076
  8.7 6.6 copy-start.32
  8.7 6.7 copy-start.30
  12.1 153.4 %all-reduce.9.cloned.1.call-start = ((), (), s32[]{:S(2)}) async-start(), calls=%async_computation.10 | async-start | bytes 131072 | tf_op jit(solution)/shard_map/psum | solution.py:162
  112.8 229.5 %reduce-scatter.10.cloned.1.call-start = ((), (), s32[]{:S(2)}) async-start(), calls=%async_computation.11 | async-start | bytes 9437184 | tf_op jit(solution)/shard_map/reduce_scatter | solution.py:185
  271.5 73.7 %copy-start.29 = (f32[1024]{0:T(1024)S(1)}, f32[1024]{0:T(1024)}, u32[]{:S(2)}) copy-start(f32[1024]{0:T(1024)} %param.45) | copy-start | bytes 12292
  271.5 133.3 %all-gather.5.cloned.1.call-start = ((), (), s32[]{:S(2)}) async-start(), calls=%async_computation.12 | async-start | bytes 4718592 | tf_op jit(solution)/shard_map/all_gather | solution.py:212
  342.3 9.4 slice-start
  345.1 19.9 %copy-start.6 = (f32[256,1024]{1,0:T(8,128)}, f32[256,1024]{1,0:T(8,128)S(1)}, u32[]{:S(2)}) copy-start(f32[256,1024]{1,0:T(8,128)S(1)} %get-tuple-element.1028) | copy-start | bytes 3145732
  345.3 6.3 copy-start.10
  345.3 6.3 slice-start.1
  345.4 9.6 slice-start.4
  351.7 3.3 copy-start.15
  351.7 3.3 slice-start.5
  351.7 10.9 slice-start.2
  355.0 7.6 slice-start.3
  360.9 1.7 copy-start.16
  360.9 1.7 copy-start.17
  362.6 3.7 copy-start.7
  367.9 140.2 %all-reduce.11.cloned.1.call-start = ((), (), s32[]{:S(2)}) async-start(), calls=%async_computation.13 | async-start | bytes 131072 | tf_op jit(solution)/shard_map/psum | solution.py:241
  408.0 2.9 copy-start.23
  455.4 261.9 %reduce-scatter.12.cloned.1.call-start = ((), (), s32[]{:S(2)}) async-start(), calls=%async_computation.14 | async-start | bytes 9437184 | tf_op jit(solution)/shard_map/reduce_scatter | solution.py:299
  508.0 4.2 copy-start.24
  573.8 2.5 copy-start.11
  573.8 2.8 copy-start.21
  578.2 2.2 copy-start.22
  578.2 2.2 copy-start.1
  582.4 2.1 copy-start.2
  586.3 2.5 copy-start.11
  586.4 2.8 copy-start.21
  590.8 2.2 copy-start.22
  590.8 2.2 copy-start.1
  595.0 2.0 copy-start.2
  598.9 2.5 copy-start.11
  598.9 2.8 copy-start.21
  603.3 2.2 copy-start.22
  603.3 2.2 copy-start.1
  607.5 2.1 copy-start.2
  611.5 2.5 copy-start.11
  611.5 2.8 copy-start.21
  615.9 2.2 copy-start.22
  615.9 2.2 copy-start.1
  620.1 2.1 copy-start.2
  646.5 125.5 %reduce-scatter.20.cloned.1.call-start = ((), (), s32[]{:S(2)}) async-start(), calls=%async_computation.18 | async-start | bytes 4718592 | tf_op jit(solution)/shard_map/reduce_scatter | solution.py:317
  651.0 1.7 copy-start.28
  651.0 176.2 %reduce-scatter.18.cloned.1.call-start = ((), (), s32[]{:S(2)}) async-start(), calls=%async_computation.17 | async-start | bytes 4718592 | tf_op jit(solution)/shard_map/reduce_scatter | solution.py:316
  655.9 226.0 %reduce-scatter.16.cloned.1.call-start = ((), (), s32[]{:S(2)}) async-start(), calls=%async_computation.16 | async-start | bytes 4718592 | tf_op jit(solution)/shard_map/reduce_scatter | solution.py:315
  661.2 311.2 %reduce-scatter.24.cloned.1.call-start = ((), (), s32[]{:S(2)}) async-start(), calls=%async_computation.20 | async-start | bytes 12976128 | tf_op jit(solution)/shard_map/reduce_scatter | solution.py:320
  669.1 394.0 %reduce-scatter.22.cloned.1.call-start = ((), (), s32[]{:S(2)}) async-start(), calls=%async_computation.19 | async-start | bytes 12976128 | tf_op jit(solution)/shard_map/reduce_scatter | solution.py:319
  676.7 477.0 %reduce-scatter.26.cloned.1.call-start = ((), (), s32[]{:S(2)}) async-start(), calls=%async_computation.21 | async-start | bytes 12976128 | tf_op jit(solution)/shard_map/reduce_scatter | solution.py:321
  684.3 524.4 %reduce-scatter.14.cloned.1.call-start = ((), (), s32[]{:S(2)}) async-start(), calls=%async_computation.15 | async-start | bytes 4718592 | tf_op jit(solution)/shard_map/reduce_scatter | solution.py:314
  721.4 487.3 %copy-start.33 = (u32[32]{0:T(128)S(1)}, u32[32]{0:T(128)}, u32[]{:S(2)}) copy-start(u32[32]{0:T(128)} %constant.261) | copy-start | bytes 388
  721.4 719.5 %all-reduce.13.cloned.1.call-start = ((), (), s32[]{:S(2)}) async-start(), calls=%async_computation.22 | async-start | bytes 12845056 | tf_op jit(solution)/shard_map/psum | solution.py:334
  1210.0 5.9 copy-start.12
  1210.0 5.9 copy-start.13
  1215.9 2.4 copy-start.14
  1218.4 2.7 copy-start.31
  1440.9 7.8 copy-start.20
  1440.9 8.9 copy-start.19
  1443.0 8.0 copy-start.18
  (5 other events, 6.2 us)
Sparse Core Ops, SparseCore 0:
  12.2 39.4 all-gather.2
  112.9 52.4 all-reduce.8
  271.6 70.6 reduce-scatter.9
  368.0 36.7 all-gather.4
  455.5 52.4 all-reduce.10
  646.7 70.6 reduce-scatter.11
  720.7 51.3 reduce-scatter.19
  775.8 51.3 reduce-scatter.17
  830.5 51.2 reduce-scatter.15
  885.6 86.7 reduce-scatter.23
  976.3 86.7 reduce-scatter.21
  1066.9 86.7 reduce-scatter.25
  1157.4 51.2 reduce-scatter.13
  1211.5 229.3 all-reduce.12
where the time goes:
time: 1470 us; the launch traced here: 1460 us
  waiting for transfers between devices  927 us (63%)
  matrix products  254 us (17%)
  local copies, waits for them, and re-layouts  149 us (10%)
  blocking collectives  49.1 us (3%)
  other arithmetic  39.6 us (3%)
  loops' own time  23.4 us (2%)
  between operations  16.1 us (1%)
    psum x1, waiting for transfers between devices, local(): lax.psum((norm_part, query_part, key_part, value_part, out_part, ffn_gain...  191 us
    reduce_scatter x1, waiting for transfers between devices, local(): lax.psum_scatter(gate_grad, 'mem', scatter_dimension=0, tiled=True)  90.7 us
    reduce_scatter x1, waiting for transfers between devices, local(): lax.psum_scatter(up_grad, 'mem', scatter_dimension=0, tiled=True)  90.6 us
    reduce_scatter x1, waiting for transfers between devices, local(): lax.psum_scatter(down_grad, 'mem', scatter_dimension=0, tiled=True)  90.5 us
    reduce_scatter x1, waiting for transfers between devices, local(): lax.psum_scatter(numerators.reshape(all_rows, model_width), 'mem', scatte...  70.8 us
    reduce_scatter x1, waiting for transfers between devices, local(): lax.psum_scatter(value_grad, 'mem', scatter_dimension=0, tiled=True)  55.1 us
    reduce_scatter x1, waiting for transfers between devices, local(): lax.psum_scatter(query_grad, 'mem', scatter_dimension=0, tiled=True)  55 us
    reduce_scatter x1, waiting for transfers between devices, local(): lax.psum_scatter(key_grad, 'mem', scatter_dimension=0, tiled=True)  54.7 us
  transfers between devices with their start and end apart: 14, of which 14 were waited for; matrix products, arithmetic and copies ran while one was open for 6% of the time, Pallas kernels for 0%

commit v1 on v0

--- a/solution.py
+++ b/solution.py
@@ -209,7 +209,9 @@
     d_res_low = d_res.astype(jnp.bfloat16)
     out_grad = outer_product(attended, d_res_low)
     d_att = backward_dot(d_res_low, w_out).astype(jnp.bfloat16)
-    grad_rows = lax.all_gather(d_att, "mem", axis=0, tiled=True).reshape(blocks, QB, H, HD)
+    grad_rows = jnp.concatenate(
+        lax.all_to_all(jnp.stack([d_att] * lax.axis_size("mem")), "mem", 0, 0), axis=0
+    ).reshape(blocks, QB, H, HD)
 
     def memory_third(pieces):
         query_block, key_block, value_block, usable, block_total, grad_block = pieces

time: 1470 us -> 1490 us (1.014)
    all_to_all x0 -> x1, waiting for transfers between devices: none -> 46.6 us  [local(): lax.all_to_all(jnp.stack([d_att] * lax.axis_size('mem')), 'mem', 0, 0)]
    all_gather x1 -> x0, waiting for transfers between devices: 34.3 us -> none  [local(): lax.all_gather(d_att, 'mem', axis=0, tiled=True).reshape(blocks, QB, H, HD)]
    unnamed x85 -> x99, local copies, waits for them, and re-layouts: 35.1 us -> 39.1 us
where the time goes in v1:
time: 1490 us; the launch traced here: 1480 us
  waiting for transfers between devices  936 us (63%)
  matrix products  254 us (17%)
  local copies, waits for them, and re-layouts  155 us (10%)
  blocking collectives  49.2 us (3%)
  other arithmetic  36.7 us (2%)
  loops' own time  23.4 us (2%)
  between operations  16.1 us (1%)
    psum x1, waiting for transfers between devices, local(): lax.psum((norm_part, query_part, key_part, value_part, out_part, ffn_gain...  192 us
    reduce_scatter x1, waiting for transfers between devices, local(): lax.psum_scatter(up_grad, 'mem', scatter_dimension=0, tiled=True)  90.7 us
    reduce_scatter x1, waiting for transfers between devices, local(): lax.psum_scatter(down_grad, 'mem', scatter_dimension=0, tiled=True)  90.7 us
    reduce_scatter x1, waiting for transfers between devices, local(): lax.psum_scatter(gate_grad, 'mem', scatter_dimension=0, tiled=True)  90.5 us
    reduce_scatter x1, waiting for transfers between devices, local(): lax.psum_scatter(numerators.reshape(all_rows, model_width), 'mem', scatte...  70.8 us
    reduce_scatter x1, waiting for transfers between devices, local(): lax.psum_scatter(value_grad, 'mem', scatter_dimension=0, tiled=True)  55.1 us
    reduce_scatter x1, waiting for transfers between devices, local(): lax.psum_scatter(query_grad, 'mem', scatter_dimension=0, tiled=True)  54.9 us
    reduce_scatter x1, waiting for transfers between devices, local(): lax.psum_scatter(key_grad, 'mem', scatter_dimension=0, tiled=True)  54.7 us
  transfers between devices with their start and end apart: 14, of which 14 were waited for; matrix products, arithmetic and copies ran while one was open for 6% of the time, Pallas kernels for 0%

profile of v1, /device:TPU:0, one launch (start us, length us, event | category | flops | bytes accessed | tf_op | source)
XLA Modules:
  0.0 1477.1 jit_solution(15884620019467557923)
XLA Ops:
  8.7 3.3 convolution_convert_fusion.3
  15.4 22.5 %while.110 = (s32[]{:T(128)}, bf16[4,128,1024]{2,1,0:T(8,128)(2,1)}, bf16[4,128,1024]{2,1,0:T(8,128)(2,1)}, s32[4,128]{1,0:T(4,128)S(1)}, pred[4,128]{1,0:T(4,12...) while((s32[]{:T(128)}, bf16[4,128,1024]{2,1,0:T(8,128)(2,1)}, ...), condition=%wide.region_2.3_spmd.clone, body=%wide.region_1.2_spmd.clone.sunk | while | flops 537657344 | bytes 4721261 | solution.py:114
  40.4 11.4 all-gather.2.cloned.1.call-done
  51.8 3.3 copy.137
  58.0 20.9 %while.111 = (s32[]{:T(128)}, f32[4,512,8]{1,2,0:T(8,128)S(1)}, f32[4,512,8]{1,2,0:T(8,128)S(1)}, s32[4]{0:T(128)S(1)}, pred[256]{0:T(512)(128)(4,1)S(1)}, /*ind...) while((s32[]{:T(128)}, f32[4,512,8]{1,2,0:T(8,128)S(1)}, ...), condition=%wide.region_10.11_spmd.clone, body=%wide.region_7.10_spmd.clone.sunk | while | flops 277078784 | bytes 10475995 | solution.py:155
  78.9 9.8 while.106
  88.7 23.5 %pmax.7 = bf16[4,512,8]{1,2,0:T(8,128)(2,1)S(1)} all-reduce(bf16[4,512,8]{1,2,0:T(8,128)(2,1)S(1)} %get-tuple-element.1010), channel_id=1, replica_groups=mesh['seg'=4,'mem'=8] {'mem'}, use_global_device_ids=true, to_apply=%region_11.12 | all-reduce | flops 16384 | bytes 65536 | tf_op jit(solution)/shard_map/pmax | solution.py:161
  119.3 46.3 %all-reduce.9.cloned.1.call-done = f32[4,512,8]{1,2,0:T(8,128)} async-done(((f32[4,512,8]{1,2,0:T(8,128)}), f32[4,512,8]{1,2,0:T(8,128)}) %all-reduce.9.cloned.1.call-update) | async-done | bytes 65552 | tf_op jit(solution)/shard_map/psum | solution.py:162
  166.4 4.3 broadcast.313.clone3.1
  170.7 26.3 %while.112 = (s32[]{:T(128)}, f32[4,512,8,128]{3,1,2,0:T(8,128)}, s32[4]{0:T(128)S(1)}, pred[256]{0:T(512)(128)(4,1)S(1)}, s32[]{:T(128)}, /*index=5*/bf16[4,512...) while((s32[]{:T(128)}, f32[4,512,8,128]{3,1,2,0:T(8,128)}, ...), condition=%wide.region_16.17_spmd.clone, body=%wide.region_15.16_spmd.clone.sunk | while | flops 542376704 | bytes 4643303 | solution.py:184
  172.8 4.5 bitcast_dynamic-update-slice_fusion.17
  179.3 4.4 bitcast_dynamic-update-slice_fusion.17
  185.9 4.5 bitcast_dynamic-update-slice_fusion.17
  192.4 4.5 bitcast_dynamic-update-slice_fusion.17
  196.9 4.2 broadcast.313.clone3
  201.2 46.7 %while.107 = (s32[]{:T(128)}, f32[4,512,8,128]{3,1,2,0:T(8,128)}, bf16[4,128,8,128]{3,2,1,0:T(8,128)(2,1)}, pred[4,128]{1,0:T(4,128)(4,1)S(1)}, bf16[4,128,8,128...) while((s32[]{:T(128)}, f32[4,512,8,128]{3,1,2,0:T(8,128)}, ...), condition=%wide.region_14.15_spmd, body=%wide.region_13.14_spmd.sunk | while | flops 271056896 | bytes 13158765 | solution.py:173
  203.1 3.7 convolution_bitcast_fusion.2
  214.7 3.7 convolution_bitcast_fusion.2
  226.2 3.7 convolution_bitcast_fusion.2
  237.8 3.7 convolution_bitcast_fusion.2
  247.9 10.3 add.250
  258.2 8.2 copy.96
  266.4 5.4 copy.148
  271.8 70.8 %reduce-scatter.10.cloned.1.call-done = f32[256,1024]{1,0:T(8,128)} async-done(((f32[2048,1024]{1,0:T(8,128)}), f32[256,1024]{1,0:T(8,128)}) %reduce-scatter.10.cloned.1.call-update) | async-done | bytes 1048592 | tf_op jit(solution)/shard_map/reduce_scatter | solution.py:185
  345.8 6.3 fusion.216
  352.1 3.2 fusion.215
  355.4 5.9 multiply_convert_fusion
  370.0 4.5 all-to-all-start
  377.1 46.6 %all-to-all-done = bf16[8,256,1024]{2,1,0:T(8,128)(2,1)} async-done(((bf16[8,256,1024]{2,1,0:T(8,128)(2,1)}), bf16[8,256,1024]{2,1,0:T(8,128)(2,1)}, u32[]{:S(2)}, u32[]{:S(2)}) %all-to-all-start) | async-done | bytes 4194336 | tf_op jit(solution)/shard_map/all_to_all | solution.py:213
  423.7 3.3 copy.139
  429.9 28.1 %while.113 = (s32[]{:T(128)}, f32[4,512,8]{1,2,0:T(8,128)S(1)}, s32[4]{0:T(128)S(1)}, pred[256]{0:T(512)(128)(4,1)S(1)}, s32[]{:T(128)}, /*index=5*/bf16[4,512,8...) while((s32[]{:T(128)}, f32[4,512,8]{1,2,0:T(8,128)S(1)}, ...), condition=%wide.region_25.26_spmd.clone, body=%wide.region_23.25_spmd.clone.sunk | while | flops 543421184 | bytes 12032499 | solution.py:242
  458.0 15.7 %while.108 = (s32[]{:T(128)}, f32[4,512,8]{1,2,0:T(8,128)S(1)}, pred[4,128]{1,0:T(4,128)(4,1)S(1)}, bf16[4,128,8,128]{3,1,2,0:T(8,128)(2,1)}, bf16[4,512,8,128]{...) while((s32[]{:T(128)}, f32[4,512,8]{1,2,0:T(8,128)S(1)}, ...), condition=%wide.region_22.23_spmd, body=%wide.region_20.22_spmd.sunk | while | flops 271577088 | bytes 6917489 | solution.py:225
  474.4 51.7 %all-reduce.11.cloned.1.call-done = f32[4,512,8]{1,2,0:T(8,128)} async-done(((f32[4,512,8]{1,2,0:T(8,128)}), f32[4,512,8]{1,2,0:T(8,128)}) %all-reduce.11.cloned.1.call-update) | async-done | bytes 65552 | tf_op jit(solution)/shard_map/psum | solution.py:243
  526.1 4.2 broadcast.313.clone3.2
  530.3 55.5 %while.109 = (s32[]{:T(128)}, f32[4,512,8,128]{3,1,2,0:T(8,128)}, bf16[4,128,8,128]{3,1,2,0:T(8,128)(2,1)}, pred[4,128]{1,0:T(4,128)(4,1)S(1)}, bf16[4,512,8,128...) while((s32[]{:T(128)}, f32[4,512,8,128]{3,1,2,0:T(8,128)}, ...), condition=%wide.region_28.29_spmd, body=%wide.region_27.28_spmd.sunk | while | flops 407371776 | bytes 17665912 | solution.py:260
  530.6 3.1 fusion.329
  533.7 4.6 multiply_bitcast_fusion.2
  547.6 4.6 multiply_bitcast_fusion.2
  561.4 4.6 multiply_bitcast_fusion.2
  575.2 4.6 multiply_bitcast_fusion.2
  585.8 4.3 broadcast.313.clone3.3
  590.1 50.7 %while.114 = (s32[]{:T(128)}, f32[256,8,128]{0,2,1:T(8,128)}, f32[256,8,128]{0,2,1:T(8,128)}, f32[4,512,8,128]{3,1,2,0:T(8,128)}, s32[4]{0:T(128)S(1)}, /*index=...) while((s32[]{:T(128)}, f32[256,8,128]{0,2,1:T(8,128)}, ...), condition=%wide.region_30.31_spmd.clone, body=%wide.region_29.30_spmd.clone.sunk | while | flops 1357906688 | bytes 65264296 | solution.py:297
  640.8 10.3 add.259
  651.1 8.2 copy.115
  659.4 5.4 copy.147
  666.0 4.0 fusion.199
  672.1 4.3 fusion.206
  677.4 4.0 fusion.208
  681.7 7.4 fusion.219
  689.2 7.5 fusion.218
  697.7 7.5 fusion.220
  705.2 30.4 %reduce-scatter.12.cloned.1.call-done = f32[256,1024]{1,0:T(8,128)} async-done(((f32[2048,1024]{1,0:T(8,128)}), f32[256,1024]{1,0:T(8,128)}) %reduce-scatter.12.cloned.1.call-update) | async-done | bytes 1048592 | tf_op jit(solution)/shard_map/reduce_scatter | solution.py:301
  735.6 4.0 fusion.195
  739.8 50.5 %reduce-scatter.20.cloned.1.call-done = f32[128,1024]{1,0:T(8,128)} async-done(((f32[1024,1024]{1,0:T(8,128)}), f32[128,1024]{1,0:T(8,128)}) %reduce-scatter.20.cloned.1.call-update) | async-done | bytes 524304 | tf_op jit(solution)/shard_map/reduce_scatter | solution.py:319
  790.2 55.1 %reduce-scatter.18.cloned.1.call-done = f32[128,1024]{1,0:T(8,128)} async-done(((f32[1024,1024]{1,0:T(8,128)}), f32[128,1024]{1,0:T(8,128)}) %reduce-scatter.18.cloned.1.call-update) | async-done | bytes 524304 | tf_op jit(solution)/shard_map/reduce_scatter | solution.py:318
  845.3 54.7 %reduce-scatter.16.cloned.1.call-done = f32[128,1024]{1,0:T(8,128)} async-done(((f32[1024,1024]{1,0:T(8,128)}), f32[128,1024]{1,0:T(8,128)}) %reduce-scatter.16.cloned.1.call-update) | async-done | bytes 524304 | tf_op jit(solution)/shard_map/reduce_scatter | solution.py:317
  900.0 90.7 %reduce-scatter.24.cloned.1.call-done = f32[128,2816]{1,0:T(8,128)} async-done(((f32[1024,2816]{1,0:T(8,128)}), f32[128,2816]{1,0:T(8,128)}) %reduce-scatter.24.cloned.1.call-update) | async-done | bytes 1441808 | tf_op jit(solution)/shard_map/reduce_scatter | solution.py:322
  990.7 90.5 %reduce-scatter.22.cloned.1.call-done = f32[128,2816]{1,0:T(8,128)} async-done(((f32[1024,2816]{1,0:T(8,128)}), f32[128,2816]{1,0:T(8,128)}) %reduce-scatter.22.cloned.1.call-update) | async-done | bytes 1441808 | tf_op jit(solution)/shard_map/reduce_scatter | solution.py:321
  1081.2 90.7 %reduce-scatter.26.cloned.1.call-done = f32[352,1024]{1,0:T(8,128)} async-done(((f32[2816,1024]{1,0:T(8,128)}), f32[352,1024]{1,0:T(8,128)}) %reduce-scatter.26.cloned.1.call-update) | async-done | bytes 1441808 | tf_op jit(solution)/shard_map/reduce_scatter | solution.py:323
  1171.9 54.9 %reduce-scatter.14.cloned.1.call-done = f32[128,1024]{1,0:T(8,128)} async-done(((f32[1024,1024]{1,0:T(8,128)}), f32[128,1024]{1,0:T(8,128)}) %reduce-scatter.14.cloned.1.call-update) | async-done | bytes 524304 | tf_op jit(solution)/shard_map/reduce_scatter | solution.py:316
  1228.2 5.9 fusion.184
  1239.2 13.2 all-reduce.2
  1252.5 12.5 all-reduce.3
  1267.7 191.5 %all-reduce.13.cloned.1.call-done = (f32[128,1024]{1,0:T(8,128)}, f32[128,1024]{1,0:T(8,128)}, f32[128,1024]{1,0:T(8,128)}, f32[128,1024]{1,0:T(8,128)}, f32[128...) async-done(((f32[128,1024]{1,0:T(8,128)}, f32[128,1024]{1,0:T(8,128)}, f32[128,1024]{1,0:T(8,128)}, f32[128,1024]{1,0:T(8,128)}, f32[128,2816]{1,0:T(8,128)}, ...) | async-done | bytes 6422544 | tf_op jit(solution)/shard_map/psum | solution.py:336
  (427 shorter events, 258.9 us)
Async XLA Ops:
  7.2 106.1 %copy-start = (bf16[1024,1024]{1,0:T(8,128)(2,1)S(1)}, bf16[1024,1024]{1,0:T(8,128)(2,1)}, u32[]{:S(2)}) copy-start(bf16[1024,1024]{1,0:T(8,128)(2,1)} %param.43) | copy-start | bytes 6291460
  7.2 5.6 copy-start.4
  7.2 5.6 copy-start.32
  7.2 44.5 %all-gather.2.cloned.1.call-start = ((), (), s32[]{:S(2)}) async-start(), calls=%async_computation.10 | async-start | bytes 4718592 | tf_op jit(solution)/shard_map/all_gather | solution.py:115
  8.6 104.6 %copy-start.34 = (f32[256]{0:T(256)}, f32[256]{0:T(256)S(1)}, u32[]{:S(2)}) copy-start(f32[256]{0:T(256)S(1)} %add_rsqrt_fusion.1) | copy-start | bytes 3076
  8.7 6.6 copy-start.39
  8.7 6.7 copy-start.37
  12.1 153.5 %all-reduce.9.cloned.1.call-start = ((), (), s32[]{:S(2)}) async-start(), calls=%async_computation.11 | async-start | bytes 131072 | tf_op jit(solution)/shard_map/psum | solution.py:162
  112.9 229.7 %reduce-scatter.10.cloned.1.call-start = ((), (), s32[]{:S(2)}) async-start(), calls=%async_computation.12 | async-start | bytes 9437184 | tf_op jit(solution)/shard_map/reduce_scatter | solution.py:185
  271.8 73.7 %copy-start.36 = (f32[1024]{0:T(1024)S(1)}, f32[1024]{0:T(1024)}, u32[]{:S(2)}) copy-start(f32[1024]{0:T(1024)} %param.45) | copy-start | bytes 12292
  342.7 9.4 slice-start
  345.5 19.8 %copy-start.8 = (f32[256,1024]{1,0:T(8,128)}, f32[256,1024]{1,0:T(8,128)S(1)}, u32[]{:S(2)}) copy-start(f32[256,1024]{1,0:T(8,128)S(1)} %get-tuple-element.1028) | copy-start | bytes 3145732
  345.7 6.3 copy-start.14
  345.7 6.3 slice-start.1
  345.8 9.6 slice-start.4
  352.1 3.3 copy-start.20
  352.1 3.3 slice-start.5
  352.1 10.8 slice-start.2
  355.3 7.6 slice-start.3
  363.0 3.7 copy-start.9
  370.0 53.7 %all-to-all-start = ((bf16[8,256,1024]{2,1,0:T(8,128)(2,1)}), bf16[8,256,1024]{2,1,0:T(8,128)(2,1)}, u32[]{:S(2)}, u32[]{:S(2)}) async-start(bf16[8,256,1024]{2,1,0:T(8,128)(2,1)} %stack.2), calls=%async_computation.1 | async-start | bytes 8388608 | tf_op jit(solution)/shard_map/all_to_all | solution.py:213
  374.5 151.6 %all-reduce.11.cloned.1.call-start = ((), (), s32[]{:S(2)}) async-start(), calls=%async_computation.13 | async-start | bytes 131072 | tf_op jit(solution)/shard_map/psum | solution.py:243
  427.0 2.9 copy-start.30
  474.4 261.3 %reduce-scatter.12.cloned.1.call-start = ((), (), s32[]{:S(2)}) async-start(), calls=%async_computation.14 | async-start | bytes 9437184 | tf_op jit(solution)/shard_map/reduce_scatter | solution.py:301
  526.1 4.2 copy-start.31
  592.0 2.5 copy-start.16
  592.0 2.8 copy-start.27
  596.4 2.2 copy-start.28
  596.4 2.2 copy-start.1
  604.5 2.5 copy-start.16
  604.5 2.8 copy-start.27
  609.0 2.2 copy-start.28
  609.0 2.2 copy-start.1
  617.1 2.5 copy-start.16
  617.1 2.8 copy-start.27
  621.5 2.2 copy-start.28
  621.5 2.2 copy-start.1
  625.7 2.1 copy-start.2
  629.7 2.5 copy-start.16
  629.7 2.8 copy-start.27
  634.1 2.2 copy-start.28
  634.1 2.2 copy-start.1
  638.3 2.1 copy-start.2
  664.8 125.4 %reduce-scatter.20.cloned.1.call-start = ((), (), s32[]{:S(2)}) async-start(), calls=%async_computation.18 | async-start | bytes 4718592 | tf_op jit(solution)/shard_map/reduce_scatter | solution.py:319
  670.0 2.1 copy-start.35
  670.1 175.2 %reduce-scatter.18.cloned.1.call-start = ((), (), s32[]{:S(2)}) async-start(), calls=%async_computation.17 | async-start | bytes 4718592 | tf_op jit(solution)/shard_map/reduce_scatter | solution.py:318
  672.1 4.4 copy-start.3
  676.5 223.5 %reduce-scatter.16.cloned.1.call-start = ((), (), s32[]{:S(2)}) async-start(), calls=%async_computation.16 | async-start | bytes 4718592 | tf_op jit(solution)/shard_map/reduce_scatter | solution.py:317
  677.4 4.3 copy-start.15
  681.5 309.2 %reduce-scatter.24.cloned.1.call-start = ((), (), s32[]{:S(2)}) async-start(), calls=%async_computation.20 | async-start | bytes 12976128 | tf_op jit(solution)/shard_map/reduce_scatter | solution.py:322
  689.1 392.1 %reduce-scatter.22.cloned.1.call-start = ((), (), s32[]{:S(2)}) async-start(), calls=%async_computation.19 | async-start | bytes 12976128 | tf_op jit(solution)/shard_map/reduce_scatter | solution.py:321
  696.7 475.2 %reduce-scatter.26.cloned.1.call-start = ((), (), s32[]{:S(2)}) async-start(), calls=%async_computation.21 | async-start | bytes 12976128 | tf_op jit(solution)/shard_map/reduce_scatter | solution.py:323
  705.2 30.5 %copy-start.5 = (bf16[256,1024]{1,0:T(8,128)(2,1)S(1)}, bf16[256,1024]{1,0:T(8,128)(2,1)}, u32[]{:S(2)}) copy-start(bf16[256,1024]{1,0:T(8,128)(2,1)} %param.34) | copy-start | bytes 1572868
  705.2 521.7 %reduce-scatter.14.cloned.1.call-start = ((), (), s32[]{:S(2)}) async-start(), calls=%async_computation.15 | async-start | bytes 4718592 | tf_op jit(solution)/shard_map/reduce_scatter | solution.py:316
  739.7 487.2 %copy-start.40 = (u32[32]{0:T(128)S(1)}, u32[32]{0:T(128)}, u32[]{:S(2)}) copy-start(u32[32]{0:T(128)} %constant.261) | copy-start | bytes 388
  739.7 719.5 %all-reduce.13.cloned.1.call-start = ((), (), s32[]{:S(2)}) async-start(), calls=%async_computation.22 | async-start | bytes 12845056 | tf_op jit(solution)/shard_map/psum | solution.py:336
  1228.2 5.9 copy-start.17
  1228.2 5.9 copy-start.18
  1234.1 2.3 copy-start.19
  1234.1 3.1 copy-start.11
  1236.4 2.7 copy-start.38
  1459.2 7.8 copy-start.26
  1459.2 8.9 copy-start.25
  1461.3 8.0 copy-start.24
  (12 other events, 16.8 us)
Sparse Core Ops, SparseCore 0:
  12.2 39.5 all-gather.1
  113.1 52.4 all-reduce.8
  271.9 70.6 reduce-scatter.9
  474.5 51.5 all-reduce.10
  664.9 70.6 reduce-scatter.11
  738.9 51.3 reduce-scatter.19
  793.9 51.3 reduce-scatter.17
  848.7 51.2 reduce-scatter.15
  903.9 86.7 reduce-scatter.23
  994.5 86.7 reduce-scatter.21
  1085.1 86.7 reduce-scatter.25
  1175.5 51.3 reduce-scatter.13
  1229.8 229.3 all-reduce.12
